TPU v7x, 32 devices: a whole 2x2x4 slice. The times are simulated.
32 devices in a mesh: row: 8 (over y, x, core), col: 4 (over z).
Axes of the slice: x: 2, y: 2, z: 4, core: 2. Of those that a mesh axis runs over, the one named last changes fastest.
Arguments:
- col_samples: float32 [16, 2, 2048, 128], P('row', None, 'col'), may hold values from -6 to 6
- row_samples: float32 [16, 2, 128, 2048], P('row', None, None, 'col'), may hold values from -6 to 6
- pivot_rows: int32 [16, 128], P('row'), may hold values from 0 to 2047
- rank_blocks: int32 [16], P('row'), may hold values from 1 to 8
- upper_inverse: float32 [2, 2048, 2048], P(None, 'col', 'row'), as said below
- upanel_left: float32 [4, 2, 2048, 128], P('col'), may hold values from -0.125 to 0.125
Outputs:
- panel_right: float32 [16, 2, 128, 2048], P('row', None, None, 'col')
- cores: float32 [16, 4, 2, 128, 128], P('row', 'col')
Inputs may be any that keep to these rules, and one draw needn't show every extreme that they name: `rank_blocks`: the tile's rank is 16 times this. `upper_inverse`: zero below the diagonal in both parts.
All inputs are finite; a program needn't handle non-finite values.
Results may differ from a plain program's by a relative error of at most 0.00007.
Values sent between devices are 32-bit elements; how exact they have to be, the bound alone decides.
A program may use at most 64 MiB of HBM per device.

v0:
```python
import jax
import jax.numpy as jnp
from jax import lax
from jax.sharding import PartitionSpec as P

RANK_STEP = 16


def complex_product(pattern, left_real, left_imag, right_real, right_imag):

    def single(left, right):
        return jnp.einsum(
            pattern,
            left,
            right,
            precision=lax.Precision.HIGHEST,
            preferred_element_type=jnp.float32,
        )

    real_part = single(left_real, right_real) - single(left_imag, right_imag)
    imag_part = single(left_real, right_imag) + single(left_imag, right_real)
    return (real_part, imag_part)


def scale_rows(values, weight_real, weight_imag):
    wr = weight_real[:, :, None]
    wi = weight_imag[:, :, None]
    real_part = values[:, 0] * wr - values[:, 1] * wi
    imag_part = values[:, 0] * wi + values[:, 1] * wr
    return jnp.stack((real_part, imag_part), axis=1)


def on_device(col_samples, row_samples, pivot_rows, rank_blocks, upper_inverse, upanel_left):
    width_local = col_samples.shape[2]
    ranks_max = row_samples.shape[2]
    offset = lax.axis_index("col") * width_local
    positions = offset + lax.broadcasted_iota(jnp.int32, (1, 1, width_local), 2)
    hits = (pivot_rows[:, :, None] == positions).astype(jnp.float32)
    flipped = jnp.swapaxes(col_samples, 2, 3)
    partial_entries = jnp.sum(flipped * hits[:, None], axis=3)
    entries = lax.psum(partial_entries, "col")
    levels = lax.broadcasted_iota(jnp.int32, (1, ranks_max), 1)
    keeping = (levels < RANK_STEP * rank_blocks[:, None]).astype(jnp.float32)
    magnitude = jnp.maximum(entries[:, 0] * entries[:, 0] + entries[:, 1] * entries[:, 1], 1.0)
    factor_real = keeping * entries[:, 0] / magnitude
    factor_imag = -keeping * entries[:, 1] / magnitude
    scaled = scale_rows(row_samples, factor_real, factor_imag)
    portion = lax.all_gather(upper_inverse, "row", axis=2, tiled=True)
    real_part, imag_part = complex_product(
        "trk,kn->trn", scaled[:, 0], scaled[:, 1], portion[0], portion[1]
    )
    partial_panel = jnp.stack((real_part, imag_part), axis=1)
    panel_full = lax.psum(partial_panel, "col")
    core_real, core_imag = complex_product(
        "trn,jns->tjrs", panel_full[:, 0], panel_full[:, 1], upanel_left[:, 0], upanel_left[:, 1]
    )
    cores = jnp.stack((core_real, core_imag), axis=2)
    panel_local = lax.dynamic_slice_in_dim(panel_full, offset, width_local, 3)
    return (panel_local, cores)


def solution(mesh):
    in_specs = (
        P("row", None, "col", None),
        P("row", None, None, "col"),
        P("row", None),
        P("row"),
        P(None, "col", "row"),
        P("col", None, None, None),
    )
    out_specs = (P("row", None, None, "col"), P("row", "col", None, None, None))
    return jax.shard_map(
        on_device, mesh=mesh, in_specs=in_specs, out_specs=out_specs, check_vma=False
    )
```

profile of v0, /device:TPU:25, one launch (start us, length us, event | category | flops | bytes accessed | tf_op | source)
XLA Modules:
  0.0 259.4 jit_solution(7308855048611063219)
XLA Ops:
  7.2 0.0 all-gather.2.cloned.1.call-start
  7.2 0.7 all-gather.2.cloned.1.call-update
  7.9 0.0 all-reduce.2.cloned.1.call-start
  8.0 0.8 compare_convert_fusion
  8.8 0.0 copy-start.3
  8.8 1.4 fusion.20
  10.2 6.4 %psum.14 = f32[2,2,128]{2,1,0:T(2,128)S(1)} all-reduce(f32[2,2,128]{2,1,0:T(2,128)S(1)} %fusion.20), channel_id=1, replica_groups=mesh['row'=8,'col'=4] {'col'}, use_global_device_ids=true, to_apply=%region_1.0 | all-reduce | flops 512 | bytes 4096 | tf_op jit(solution)/shard_map/psum | solution.py:41
  16.6 0.7 broadcast_multiply_fusion
  17.2 0.1 select_divide_fusion
  17.3 49.8 %all-gather.2.cloned.1.call-done = f32[2,512,2048]{2,1,0:T(8,128)} async-done(((f32[2,512,256]{2,1,0:T(8,128)}), f32[2,512,2048]{2,1,0:T(8,128)}) %all-gather.2.cloned.1.call-update) | async-done | bytes 8388624 | tf_op jit(solution)/shard_map/all_gather | solution.py:48
  67.1 0.0 copy-start
  67.1 5.9 %fusion = f32[2,128,2048]{2,1,0:T(8,128)S(1)} fusion(f32[2,512,2048]{2,1,0:T(8,128)} %all-gather.2.cloned.1.call-done, f32[2,2,128,512]{3,2,1,0:T(8,128)} %param.7, f32[2,128]{1,0:T(2,128)S(1)} %get-tuple-element.7, f32[2,128]{1,0:T(2,128)S(1)} %get-tuple-element.6), kind=kOutput, calls=%fused_computation.3 | convolution fusion | flops 3221618688 | bytes 7342080 | tf_op jit(solution)/shard_map/trk,kn->trn/dot_general | solution.py:12
  73.1 0.0 copy-done.3
  73.1 5.7 %fusion.1 = f32[2,128,2048]{2,1,0:T(8,128)S(1)} fusion(f32[2,512,2048]{2,1,0:T(8,128)} %all-gather.2.cloned.1.call-done, f32[2,2,128,512]{3,2,1,0:T(8,128)S(1)} %copy-done.3, f32[2,128]{1,0:T(2,128)S(1)} %get-tuple-element.7, f32[2,128]{1,0:T(2,128)S(1)} %get-tuple-element.6), kind=kOutput, calls=%fused_computation.4 | convolution fusion | flops 3221618688 | bytes 7342080 | tf_op jit(solution)/shard_map/trk,kn->trn/dot_general | solution.py:12
  78.8 0.0 copy-done
  78.8 3.8 %fusion.7 = f32[2,1,128,2048]{3,2,0,1:T(8,128)S(1)} fusion(f32[2,128,2048]{2,1,0:T(8,128)S(1)} %fusion, f32[2,512,2048]{2,1,0:T(8,128)S(1)} %copy-done, f32[2,2,128,512]{3,2,1,0:T(8,128)S(1)} %copy-done.3, f32[2,128]{1,0:T(2,128)S(1)} %get-tuple-element.7, f32[2,128]{1,0:T(2,128)S(1)} %get-tuple-element.6), kind=kOutput, calls=%fused_computation.10 | convolution fusion | flops 3222142976 | bytes 9439232 | tf_op jit(solution)/shard_map/trk,kn->trn/dot_general | solution.py:12
  82.6 3.8 %fusion.5 = f32[2,1,128,2048]{3,2,0,1:T(8,128)S(1)} fusion(f32[2,128,2048]{2,1,0:T(8,128)S(1)} %fusion.1, f32[2,512,2048]{2,1,0:T(8,128)S(1)} %copy-done, f32[2,2,128,512]{3,2,1,0:T(8,128)S(1)} %copy-done.3, f32[2,128]{1,0:T(2,128)S(1)} %get-tuple-element.7, f32[2,128]{1,0:T(2,128)S(1)} %get-tuple-element.6), kind=kOutput, calls=%fused_computation.8 | convolution fusion | flops 3222142976 | bytes 9439232 | tf_op jit(solution)/shard_map/trk,kn->trn/dot_general | solution.py:12
  86.4 2.5 pad_maximum_fusion
  88.9 0.0 copy-start.2
  88.9 0.0 all-reduce.2.cloned.1.call-update
  88.9 152.6 %all-reduce.2.cloned.1.call-done = f32[2,2,128,2048]{3,2,0,1:T(8,128)} async-done(((f32[2,2,128,2048]{3,2,0,1:T(8,128)}), f32[2,2,128,2048]{3,2,0,1:T(8,128)}) %all-reduce.2.cloned.1.call-update) | async-done | bytes 4194320 | tf_op jit(solution)/shard_map/psum | solution.py:53
  241.6 0.0 copy-start.1
  241.6 1.4 constant_dynamic-slice_fusion
  243.0 1.0 copy.11
  244.0 0.0 copy-done.2
  244.0 0.1 copy-done.1
  244.2 1.8 fusion.8
  246.0 1.8 fusion.9
  247.8 2.1 fusion.15
  249.9 1.8 fusion.13
  251.8 0.7 copy.12
  (3 shorter events, 0.0 us)
Async XLA Ops:
  7.2 60.0 %all-gather.2.cloned.1.call-start = ((), (), s32[]{:S(2)}) async-start(), calls=%async_computation | async-start | bytes 9437184 | tf_op jit(solution)/shard_map/all_gather | solution.py:48
  7.9 233.7 %all-reduce.2.cloned.1.call-start = ((), (), s32[]{:S(2)}) async-start(), calls=%async_computation.1 | async-start | bytes 8388608 | tf_op jit(solution)/shard_map/psum | solution.py:53
  8.8 64.3 %copy-start.3 = (f32[2,2,128,512]{3,2,1,0:T(8,128)S(1)}, f32[2,2,128,512]{3,2,1,0:T(8,128)}, u32[]{:S(2)}) copy-start(f32[2,2,128,512]{3,2,1,0:T(8,128)} %param.7) | copy-start | bytes 3145732
  67.1 11.7 %copy-start = (f32[2,512,2048]{2,1,0:T(8,128)S(1)}, f32[2,512,2048]{2,1,0:T(8,128)}, u32[]{:S(2)}) copy-start(f32[2,512,2048]{2,1,0:T(8,128)} %all-gather.2.cloned.1.call-done) | copy-start | bytes 25165828
  88.9 155.1 %copy-start.2 = (f32[1,2,2048,128]{3,2,1,0:T(8,128)S(1)}, f32[1,2,2048,128]{3,2,1,0:T(8,128)}, u32[]{:S(2)}) copy-start(f32[1,2,2048,128]{3,2,1,0:T(8,128)} %param.11) | copy-start | bytes 6291460
  241.6 2.6 %copy-start.1 = (f32[2,2,128,2048]{3,2,0,1:T(8,128)S(1)}, f32[2,2,128,2048]{3,2,0,1:T(8,128)}, u32[]{:S(2)}) copy-start(f32[2,2,128,2048]{3,2,0,1:T(8,128)} %all-reduce.2.cloned.1.call-done) | copy-start | bytes 12582916
Sparse Core Ops, SparseCore 0:
  9.8 57.2 all-gather.1
  89.1 152.4 all-reduce.1
where the time goes:
time: 263 us; the launch traced here: 259 us
  waiting for transfers between devices  203 us (77%)
  matrix products  26.8 us (10%)
  between operations  14.2 us (5%)
  blocking collectives  6.39 us (2%)
  other arithmetic  5.43 us (2%)
  local copies, waits for them, and re-layouts  3.36 us (1%)
    psum x1, waiting for transfers between devices, on_device(): panel_full = lax.psum(partial_panel, 'col')  153 us
    all_gather x1, waiting for transfers between devices, on_device(): portion = lax.all_gather(upper_inverse, 'row', axis=2, tiled=True)  49.8 us
    dot_general x8, matrix products, single(): jnp.einsum(pattern, left, right, precision=lax.Precision.HIGHEST, preferr...  26.8 us
    psum x1, blocking collectives, on_device(): entries = lax.psum(partial_entries, 'col')  6.39 us
  transfers between devices with their start and end apart: 2, of which 2 were waited for; matrix products, arithmetic and copies ran while one was open for 1% of the time, Pallas kernels for 0%

commit v1 on v0

v1 whole, which is shorter than its diff:
```python
import functools
import math

import jax
import jax.numpy as jnp
from jax import lax
from jax.experimental import pallas as pl
from jax.experimental.pallas import tpu as pltpu
from jax.sharding import PartitionSpec as P

RANK_STEP = 16
MESH = pl.DeviceIdType.MESH


def split(x):
    high = x.astype(jnp.bfloat16)
    low = (x - high.astype(jnp.float32)).astype(jnp.bfloat16)
    return high, low


def dot3(xh, xl, uh, ul):
    def single(a, b):
        return jnp.dot(a, b, preferred_element_type=jnp.float32)

    return single(xh, uh) + (single(xh, ul) + single(xl, uh))


def kernel(
    n_rows, n_cols,
    row_ref, u_ref, up_ref, col_ref, piv_ref, rank_ref,
    panel_ref, cores_ref,
    xh, xl, us, ps, pr, fin, lz, lg, ks, kr, eb,
    u_loc, u_send, u_sib, u_fwd, u_recv,
    p_send, p_recv,
    lz_loc, lz_send, lz_recv, lg_loc, lg_send, lg_sib, lg_fwd, lg_recv,
    k_send, k_recv, e_send, e_recv,
):
    r, c = lax.axis_index("row"), lax.axis_index("col")
    chips = n_rows // 2
    nx = math.isqrt(chips)
    ny = chips // nx
    q, h = r // 2, r % 2
    qy, qx = q // nx, q % nx
    tiles, _, ranks, wc = row_ref.shape
    nsub, sw = us.shape[1], us.shape[4]
    wq = lz.shape[1]
    half = tiles * ranks
    sib = (q * 2 + 1 - h, c)

    def ahead(d):
        return ((qy + d // nx) % ny) * nx + (qx + d % nx) % nx

    def behind(d):
        return ((qy + ny - d // nx) % ny) * nx + (qx + nx - d % nx) % nx

    def rcopy(src, dst, ssem, rsem, dev):
        return pltpu.make_async_remote_copy(
            src_ref=src, dst_ref=dst, send_sem=ssem, recv_sem=rsem, device_id=dev, device_id_type=MESH
        )

    def u_out(d, s):
        return rcopy(
            u_ref.at[:, :, s * sw:(s + 1) * sw], us.at[r, s], u_send.at[d, s], u_recv.at[r, s],
            (behind(d) * 2 + h, c),
        )

    def u_side(s):
        return rcopy(u_ref.at[:, :, s * sw:(s + 1) * sw], us.at[r, s], u_sib.at[s], u_recv.at[r, s], sib)

    def u_forward(d, s, b):
        return rcopy(us.at[b, s], us.at[b, s], u_fwd.at[d, s], u_recv.at[b, s], sib)

    def p_up(b, s):
        return rcopy(ps.at[b, s], pr.at[b, s], p_send.at[b, s], p_recv.at[b, s], (r, c + 1))

    def lz_out(k):
        to = (c + k) % n_cols
        start = pl.multiple_of(to * wc + q * wq, wq)
        return rcopy(up_ref.at[0, h, pl.ds(start, wq), :], lz.at[c], lz_send.at[k], lz_recv.at[c], (r, to))

    def lg_out(d):
        return rcopy(lz, lg.at[h, q], lg_send.at[d], lg_recv.at[h, q], (behind(d) * 2 + h, c))

    def lg_side():
        return rcopy(lz, lg.at[h, q], lg_sib.at[0], lg_recv.at[h, q], sib)

    def lg_forward(d):
        b = ahead(d)
        return rcopy(lg.at[h, b], lg.at[h, b], lg_fwd.at[d], lg_recv.at[h, b], sib)

    def k_out(k):
        to = (c + k) % n_cols
        return rcopy(ks.at[k], kr.at[c], k_send.at[k], k_recv.at[c], (r, to))

    def e_out(k):
        return rcopy(eb.at[c], eb.at[c], e_send.at[k], e_recv.at[c], (r, (c + k) % n_cols))

    def each(first, last, body):
        lax.fori_loop(first, last, lambda i, z: (body(i), z)[1], 0)

    own = [
        pltpu.make_async_copy(u_ref.at[:, :, s * sw:(s + 1) * sw], us.at[r, s], u_loc.at[s]) for s in range(nsub)
    ]
    for copy in own:
        copy.start()
    mine = pl.multiple_of(c * wc + q * wq, wq)
    lz_own = pltpu.make_async_copy(up_ref.at[0, h, pl.ds(mine, wq), :], lz.at[c], lz_loc.at[0])
    lz_own.start()
    barrier = pltpu.get_barrier_semaphore()

    def signal(dev):
        pl.semaphore_signal(barrier, inc=1, device_id=dev, device_id_type=MESH)

    signal(sib)
    each(1, chips, lambda d: signal((behind(d) * 2 + h, c)))
    each(1, n_cols, lambda k: signal((r, (c + k) % n_cols)))
    pl.semaphore_wait(barrier, 1 + (chips - 1) + (n_cols - 1))

    early = min(3, chips)

    @pl.when(q >= c)
    def _():
        for s in range(nsub):
            u_side(s).start()

        def send(d):
            for s in range(nsub):
                u_out(d, s).start()

        each(1, early, send)

    each(1, n_cols, lambda k: lz_out(k).start())

    for i in range(tiles):
        for p in range(2):
            a, b = split(row_ref[i, p])
            at = pl.ds(p * half + i * ranks, ranks)
            xh[at, :] = a
            xl[at, :] = b

    pos = c * wc + lax.broadcasted_iota(jnp.int32, (wc, ranks), 0)
    parts = []
    for i in range(tiles):
        hit = pos == piv_ref[i:i + 1, :]
        for p in range(2):
            parts.append(jnp.sum(jnp.where(hit, col_ref[i, p], 0.0), axis=0, keepdims=True))
    parts.append(jnp.zeros((eb.shape[1] - 2 * tiles, ranks), jnp.float32))
    eb[c] = jnp.concatenate(parts, axis=0)
    each(1, n_cols, lambda k: e_out(k).start())
    for copy in own:
        copy.wait()

    total = chips * nsub * 2

    def unit(u, carry):
        d, s, e = u // (2 * nsub), (u // 2) % nsub, u % 2
        t = ahead(d)
        b = t * 2 + (h + e) % 2

        @pl.when(u == 2 * nsub)
        def _():
            lz_own.wait()
            each(1, n_cols, lambda k: rcopy(
                lz.at[(c + k) % n_cols], lz.at[(c + k) % n_cols], lz_send.at[k], lz_recv.at[(c + k) % n_cols], sib
            ).wait_recv())
            lg_side().start()
            pltpu.make_async_copy(lz, lg.at[h, q], lg_loc.at[0]).start()
            each(1, chips, lambda d2: lg_out(d2).start())

            @pl.when(q >= c)
            def _():
                def send(d2):
                    for s2 in range(nsub):
                        u_out(d2, s2).start()

                each(early, chips, send)

        @pl.when(u == total - 2 * nsub)
        def _():
            def pass_on(d2):
                o = ahead(d2)
                rcopy(lz, lg.at[h, o], lg_send.at[d2], lg_recv.at[h, o], sib).wait_recv()
                lg_forward(d2).start()

            each(1, chips, pass_on)

        @pl.when(t >= c)
        def _():
            @pl.when(jnp.logical_or(d > 0, e > 0))
            def _():
                rcopy(us.at[b, s], us.at[b, s], u_fwd.at[d, s], u_recv.at[b, s], sib).wait_recv()

            @pl.when(jnp.logical_and(d > 0, e == 0))
            def _():
                u_forward(d, s, b).start()

            ur, ui = us[b, s, 0], us[b, s, 1]
            uh, ul = split(jnp.concatenate([ur, ui], axis=1))
            prod = dot3(xh[...], xl[...], uh, ul)
            fin[0:half] = prod[:half, :sw] - prod[half:, sw:]
            fin[half:2 * half] = prod[:half, sw:] + prod[half:, :sw]

            @pl.when(c > 0)
            def _():
                rcopy(ps.at[b, s], pr.at[b, s], p_send.at[b, s], p_recv.at[b, s], sib).wait_recv()
                ps[b, s] = fin[...] + pr[b, s]

            @pl.when(c == 0)
            def _():
                ps[b, s] = fin[...]

            @pl.when(t > c)
            def _():
                p_up(b, s).start()

        return carry

    lax.fori_loop(0, total, unit, 0)

    each(1, n_cols, lambda k: rcopy(
        eb.at[(c + k) % n_cols], eb.at[(c + k) % n_cols], e_send.at[k], e_recv.at[(c + k) % n_cols], sib
    ).wait_recv())
    entries = jnp.sum(eb[...], axis=0)
    lines = []
    levels = lax.broadcasted_iota(jnp.int32, (1, ranks), 1)
    for i in range(tiles):
        er, ei = entries[2 * i:2 * i + 1], entries[2 * i + 1:2 * i + 2]
        keep = (levels < RANK_STEP * rank_ref[i]).astype(jnp.float32)
        mag = jnp.maximum(er * er + ei * ei, 1.0)
        lines.append(keep * er / mag)
        lines.append(-keep * ei / mag)
    lines.append(jnp.zeros((128 - 2 * tiles, ranks), jnp.float32))
    turned = jnp.concatenate(lines, axis=0).T
    for i in range(tiles):
        fr, fi = turned[:, 2 * i:2 * i + 1], turned[:, 2 * i + 1:2 * i + 2]
        lr, li = i * ranks, half + i * ranks
        vr, vi = [], []
        for hh in range(2):
            for s in range(nsub):
                vr.append(ps[2 * c + hh, s, lr:lr + ranks, :])
                vi.append(ps[2 * c + hh, s, li:li + ranks, :])
        vr, vi = jnp.concatenate(vr, axis=1), jnp.concatenate(vi, axis=1)
        wr = vr * fr - vi * fi
        wi = vr * fi + vi * fr
        panel_ref[i, 0] = wr
        panel_ref[i, 1] = wi
        a, b = split(wr)
        xh[lr:lr + ranks, :] = a
        xl[lr:lr + ranks, :] = b
        a, b = split(wi)
        xh[li:li + ranks, :] = a
        xl[li:li + ranks, :] = b

    pltpu.make_async_copy(lz, lg.at[h, q], lg_loc.at[0]).wait()
    each(0, chips, lambda o: rcopy(
        lz, lg.at[1 - h, o], lg_sib.at[0], lg_recv.at[1 - h, o], sib
    ).wait_recv())

    def core(k0, carry):
        k = (k0 + 1) % n_cols
        j = (c + k) % n_cols
        lr = lg[0, :, j].reshape(wc, lz.shape[2])
        li = lg[1, :, j].reshape(wc, lz.shape[2])
        rank2 = lz.shape[2]
        uh, ul = split(jnp.concatenate([lr, li], axis=1))
        prod = dot3(xh[...], xl[...], uh, ul)
        real = prod[:half, :rank2] - prod[half:, rank2:]
        imag = prod[:half, rank2:] + prod[half:, :rank2]
        for i in range(tiles):
            ks[k, i, 0] = real[i * ranks:(i + 1) * ranks]
            ks[k, i, 1] = imag[i * ranks:(i + 1) * ranks]

        @pl.when(k > 0)
        def _():
            k_out(k).start()

        return carry

    lax.fori_loop(0, n_cols, core, 0)
    cores_ref[:, 0] = ks[0]

    def gather(k):
        o = (c + k) % n_cols
        rcopy(ks.at[k], kr.at[o], k_send.at[k], k_recv.at[o], sib).wait_recv()
        cores_ref[:, 0] = cores_ref[:, 0] + kr[o]

    each(1, n_cols, gather)

    @pl.when(q >= c)
    def _():
        for s in range(nsub):
            u_side(s).wait_send()

        def left(d):
            for s in range(nsub):
                u_out(d, s).wait_send()

        each(1, chips, left)

    def rest(d):
        t = ahead(d)

        @pl.when(jnp.logical_and(t >= c, d > 0))
        def _():
            for s in range(nsub):
                u_forward(d, s, t * 2 + h).wait_send()

        @pl.when(t > c)
        def _():
            for s in range(nsub):
                for e in range(2):
                    p_up(t * 2 + e, s).wait_send()

        @pl.when(d > 0)
        def _():
            lg_out(d).wait_send()
            lg_forward(d).wait_send()

    each(0, chips, rest)
    lg_side().wait_send()

    def tail(k):
        lz_out(k).wait_send()
        k_out(k).wait_send()
        e_out(k).wait_send()

    each(1, n_cols, tail)


def on_device(n_rows, n_cols, col_samples, row_samples, pivot_rows, rank_blocks, upper_inverse, upanel_left):
    tiles, _, ranks, wc = row_samples.shape
    wr = upper_inverse.shape[2]
    left_ranks = upanel_left.shape[3]
    chips = n_rows // 2
    if chips != n_cols or wc != 2 * wr:
        raise ValueError("unsupported mesh")
    nsub = max(wr // 128, 1)
    sw = wr // nsub
    wq = wc // chips
    m = 2 * tiles * ranks
    f32, bf16 = jnp.float32, jnp.bfloat16
    dma = pltpu.SemaphoreType.DMA
    vmem = pl.BlockSpec(memory_space=pltpu.VMEM)
    hbm = pl.BlockSpec(memory_space=pl.ANY)
    return pl.pallas_call(
        functools.partial(kernel, n_rows, n_cols),
        out_shape=(
            jax.ShapeDtypeStruct((tiles, 2, ranks, wc), f32),
            jax.ShapeDtypeStruct((tiles, 1, 2, ranks, left_ranks), f32),
        ),
        in_specs=[vmem, hbm, hbm, vmem, vmem, pl.BlockSpec(memory_space=pltpu.SMEM)],
        out_specs=(vmem, vmem),
        scratch_shapes=[
            pltpu.VMEM((m, wc), bf16),
            pltpu.VMEM((m, wc), bf16),
            pltpu.VMEM((n_rows, nsub, 2, wc, sw), f32),
            pltpu.VMEM((n_rows, nsub, m, sw), f32),
            pltpu.VMEM((n_rows, nsub, m, sw), f32),
            pltpu.VMEM((m, sw), f32),
            pltpu.VMEM((n_cols, wq, left_ranks), f32),
            pltpu.VMEM((2, chips, n_cols, wq, left_ranks), f32),
            pltpu.VMEM((n_cols, tiles, 2, ranks, left_ranks), f32),
            pltpu.VMEM((n_cols, tiles, 2, ranks, left_ranks), f32),
            pltpu.VMEM((n_cols, -(-2 * tiles // 8) * 8, ranks), f32),
            dma((nsub,)), dma((chips, nsub)), dma((nsub,)), dma((chips, nsub)), dma((n_rows, nsub)),
            dma((n_rows, nsub)), dma((n_rows, nsub)),
            dma((1,)), dma((n_cols,)), dma((n_cols,)), dma((1,)), dma((chips,)), dma((1,)), dma((chips,)),
            dma((2, chips)),
            dma((n_cols,)), dma((n_cols,)), dma((n_cols,)), dma((n_cols,)),
        ],
        compiler_params=pltpu.CompilerParams(
            collective_id=0, has_side_effects=True, vmem_limit_bytes=56 * 1024 * 1024
        ),
    )(row_samples, upper_inverse, upanel_left, col_samples, pivot_rows, rank_blocks)


def solution(mesh):
    in_specs = (
        P("row", None, "col", None),
        P("row", None, None, "col"),
        P("row", None),
        P("row"),
        P(None, "col", "row"),
        P("col", None, None, None),
    )
    out_specs = (P("row", None, None, "col"), P("row", "col", None, None, None))
    body = functools.partial(on_device, mesh.shape["row"], mesh.shape["col"])
    return jax.shard_map(body, mesh=mesh, in_specs=in_specs, out_specs=out_specs, check_vma=False)
```

time: 263 us -> 136 us (0.52)
  the two profiles are of different devices: /device:TPU:25 before, /device:TPU:16 now
where the time goes in v1:
time: 136 us; the launch traced here: 135 us
  Pallas kernels  132 us (97%)
  local copies, waits for them, and re-layouts  3.01 us (2%)
    pallas_call x1, Pallas kernels, on_device(): pl.pallas_call(functools.partial(kernel, n_rows, n_cols), out_shape=(jax....  132 us
    unnamed x4, local copies, waits for them, and re-layouts  3.01 us

profile of v1, /device:TPU:16, one launch (start us, length us, event | category | flops | bytes accessed | tf_op | source)
XLA Modules:
  0.0 135.4 jit_solution(3946101672994296145)
XLA Ops:
  0.6 131.7 %shard_map.77 = (f32[2,2,128,512]{3,2,1,0:T(8,128)}, f32[2,1,2,128,128]{4,3,2,1,0:T(8,128)}) custom-call(f32[2,2,128,512]{3,2,1,0:T(8,128)} %row_ref.1, f32[2,512,256]{2,1,0:T(8,128)} %u_ref.1, f32[1,2,2048,128]{3,2,1,0:T(8,128)} %up_ref.1, f32[2,2,512,128]{3,2,1,0:T(8,128)} %col_ref.1, s32[2,128]{1,0:T(2,128)} %piv_ref.1, s32[2]{0:T(128)} %rank_ref.1), custom_call_target="tpu_custom_call" | custom-call | tf_op jit(solution)/shard_map/pallas_call | solution.py:345
  132.4 0.0 copy-start
  132.4 2.3 %copy.10 = f32[2,2,128,512]{3,2,1,0:T(8,128)} copy(f32[2,2,128,512]{3,2,1,0:T(8,128)} %get-tuple-element.4) | data formatting | bytes 2097152
  134.7 0.0 copy-done
  134.7 0.7 copy.11
Async XLA Ops:
  132.4 2.3 %copy-start = (f32[2,1,2,128,128]{4,3,2,1,0:T(8,128)S(1)}, f32[2,1,2,128,128]{4,3,2,1,0:T(8,128)}, u32[]{:S(2)}) copy-start(f32[2,1,2,128,128]{4,3,2,1,0:T(8,128)} %get-tuple-element.5) | copy-start | bytes 786436

commit v2 on v1

--- a/solution.py
+++ b/solution.py
@@ -29,7 +29,7 @@
     n_rows, n_cols,
     row_ref, u_ref, up_ref, col_ref, piv_ref, rank_ref,
     panel_ref, cores_ref,
-    xh, xl, us, ps, pr, fin, lz, lg, ks, kr, eb,
+    xh, xl, ch, cl, us, ps, pr, fin, lz, lg, ks, kr, eb,
     u_loc, u_send, u_sib, u_fwd, u_recv,
     p_send, p_recv,
     lz_loc, lz_send, lz_recv, lg_loc, lg_send, lg_sib, lg_fwd, lg_recv,
@@ -67,8 +67,8 @@
     def u_side(s):
         return rcopy(u_ref.at[:, :, s * sw:(s + 1) * sw], us.at[r, s], u_sib.at[s], u_recv.at[r, s], sib)
 
-    def u_forward(d, s, b):
-        return rcopy(us.at[b, s], us.at[b, s], u_fwd.at[d, s], u_recv.at[b, s], sib)
+    def u_forward(t, s, b):
+        return rcopy(us.at[b, s], us.at[b, s], u_fwd.at[t, s], u_recv.at[b, s], sib)
 
     def p_up(b, s):
         return rcopy(ps.at[b, s], pr.at[b, s], p_send.at[b, s], p_recv.at[b, s], (r, c + 1))
@@ -123,11 +123,7 @@
         for s in range(nsub):
             u_side(s).start()
 
-        def send(d):
-            for s in range(nsub):
-                u_out(d, s).start()
-
-        each(1, early, send)
+        each(1, early, lambda d: u_out(d, 0).start())
 
     each(1, n_cols, lambda k: lz_out(k).start())
 
@@ -151,13 +147,88 @@
         copy.wait()
 
     total = chips * nsub * 2
+    per = 2 * (chips - 1)
+    own_end = 2 * nsub
+    last_phase = own_end + (nsub - 1) * per
+    spread_at = jnp.where(c == 0, own_end, 1)
+    final_at = last_phase + jnp.where(
+        q == c, 0, 2 * jnp.where(c > q, chips - 1 - c, chips - 2 - c) + 1
+    )
+    final_at = jnp.where(c == 0, total, final_at)
+
+    def finish():
+        each(1, n_cols, lambda k: rcopy(
+            eb.at[(c + k) % n_cols], eb.at[(c + k) % n_cols], e_send.at[k], e_recv.at[(c + k) % n_cols], sib
+        ).wait_recv())
+        entries = jnp.sum(eb[...], axis=0)
+        lines = []
+        levels = lax.broadcasted_iota(jnp.int32, (1, ranks), 1)
+        for i in range(tiles):
+            er, ei = entries[2 * i:2 * i + 1], entries[2 * i + 1:2 * i + 2]
+            keep = (levels < RANK_STEP * rank_ref[i]).astype(jnp.float32)
+            mag = jnp.maximum(er * er + ei * ei, 1.0)
+            lines.append(keep * er / mag)
+            lines.append(-keep * ei / mag)
+        lines.append(jnp.zeros((128 - 2 * tiles, ranks), jnp.float32))
+        turned = jnp.concatenate(lines, axis=0).T
+        for i in range(tiles):
+            fr, fi = turned[:, 2 * i:2 * i + 1], turned[:, 2 * i + 1:2 * i + 2]
+            lr, li = i * ranks, half + i * ranks
+            vr, vi = [], []
+            for hh in range(2):
+                for s in range(nsub):
+                    vr.append(ps[2 * c + hh, s, lr:lr + ranks, :])
+                    vi.append(ps[2 * c + hh, s, li:li + ranks, :])
+            vr, vi = jnp.concatenate(vr, axis=1), jnp.concatenate(vi, axis=1)
+            wr = vr * fr - vi * fi
+            wi = vr * fi + vi * fr
+            panel_ref[i, 0] = wr
+            panel_ref[i, 1] = wi
+            a, b = split(wr)
+            ch[lr:lr + ranks, :] = a
+            cl[lr:lr + ranks, :] = b
+            a, b = split(wi)
+            ch[li:li + ranks, :] = a
+            cl[li:li + ranks, :] = b
+
+        pltpu.make_async_copy(lz, lg.at[h, q], lg_loc.at[0]).wait()
+        each(0, chips, lambda o: rcopy(
+            lz, lg.at[1 - h, o], lg_sib.at[0], lg_recv.at[1 - h, o], sib
+        ).wait_recv())
+
+        def core(k0, carry):
+            k = (k0 + 1) % n_cols
+            j = (c + k) % n_cols
+            lr = lg[0, :, j].reshape(wc, lz.shape[2])
+            li = lg[1, :, j].reshape(wc, lz.shape[2])
+            rank2 = lz.shape[2]
+            uh, ul = split(jnp.concatenate([lr, li], axis=1))
+            prod = dot3(ch[...], cl[...], uh, ul)
+            real = prod[:half, :rank2] - prod[half:, rank2:]
+            imag = prod[:half, rank2:] + prod[half:, :rank2]
+            for i in range(tiles):
+                ks[k, i, 0] = real[i * ranks:(i + 1) * ranks]
+                ks[k, i, 1] = imag[i * ranks:(i + 1) * ranks]
+
+            @pl.when(k > 0)
+            def _():
+                k_out(k).start()
+
+            return carry
+
+        lax.fori_loop(0, n_cols, core, 0)
 
     def unit(u, carry):
-        d, s, e = u // (2 * nsub), (u // 2) % nsub, u % 2
-        t = ahead(d)
+        later = jnp.maximum(u - own_end, 0)
+        index = (later // 2) % (chips - 1)
+        down = chips - 1 - index
+        down = jnp.where(down > q, down, down - 1)
+        t = jnp.where(u < own_end, q, jnp.where(u < last_phase, ahead(index + 1), down))
+        s = jnp.where(u < own_end, u // 2, later // per)
+        e = u % 2
         b = t * 2 + (h + e) % 2
 
-        @pl.when(u == 2 * nsub)
+        @pl.when(u == spread_at)
         def _():
             lz_own.wait()
             each(1, n_cols, lambda k: rcopy(
@@ -169,13 +240,11 @@
 
             @pl.when(q >= c)
             def _():
-                def send(d2):
-                    for s2 in range(nsub):
-                        u_out(d2, s2).start()
-
-                each(early, chips, send)
-
-        @pl.when(u == total - 2 * nsub)
+                each(early, chips, lambda d2: u_out(d2, 0).start())
+                for s2 in range(1, nsub):
+                    each(1, chips, lambda d2: u_out(d2, s2).start())
+
+        @pl.when(u == last_phase)
         def _():
             def pass_on(d2):
                 o = ahead(d2)
@@ -184,15 +253,15 @@
 
             each(1, chips, pass_on)
 
-        @pl.when(t >= c)
-        def _():
-            @pl.when(jnp.logical_or(d > 0, e > 0))
-            def _():
-                rcopy(us.at[b, s], us.at[b, s], u_fwd.at[d, s], u_recv.at[b, s], sib).wait_recv()
-
-            @pl.when(jnp.logical_and(d > 0, e == 0))
-            def _():
-                u_forward(d, s, b).start()
+        @pl.when(jnp.logical_and(t >= c, u < total))
+        def _():
+            @pl.when(jnp.logical_or(u >= own_end, e > 0))
+            def _():
+                u_forward(t, s, b).wait_recv()
+
+            @pl.when(jnp.logical_and(u >= own_end, e == 0))
+            def _():
+                u_forward(t, s, b).start()
 
             ur, ui = us[b, s, 0], us[b, s, 1]
             uh, ul = split(jnp.concatenate([ur, ui], axis=1))
@@ -213,70 +282,13 @@
             def _():
                 p_up(b, s).start()
 
+        @pl.when(u == final_at)
+        def _():
+            finish()
+
         return carry
 
-    lax.fori_loop(0, total, unit, 0)
-
-    each(1, n_cols, lambda k: rcopy(
-        eb.at[(c + k) % n_cols], eb.at[(c + k) % n_cols], e_send.at[k], e_recv.at[(c + k) % n_cols], sib
-    ).wait_recv())
-    entries = jnp.sum(eb[...], axis=0)
-    lines = []
-    levels = lax.broadcasted_iota(jnp.int32, (1, ranks), 1)
-    for i in range(tiles):
-        er, ei = entries[2 * i:2 * i + 1], entries[2 * i + 1:2 * i + 2]
-        keep = (levels < RANK_STEP * rank_ref[i]).astype(jnp.float32)
-        mag = jnp.maximum(er * er + ei * ei, 1.0)
-        lines.append(keep * er / mag)
-        lines.append(-keep * ei / mag)
-    lines.append(jnp.zeros((128 - 2 * tiles, ranks), jnp.float32))
-    turned = jnp.concatenate(lines, axis=0).T
-    for i in range(tiles):
-        fr, fi = turned[:, 2 * i:2 * i + 1], turned[:, 2 * i + 1:2 * i + 2]
-        lr, li = i * ranks, half + i * ranks
-        vr, vi = [], []
-        for hh in range(2):
-            for s in range(nsub):
-                vr.append(ps[2 * c + hh, s, lr:lr + ranks, :])
-                vi.append(ps[2 * c + hh, s, li:li + ranks, :])
-        vr, vi = jnp.concatenate(vr, axis=1), jnp.concatenate(vi, axis=1)
-        wr = vr * fr - vi * fi
-        wi = vr * fi + vi * fr
-        panel_ref[i, 0] = wr
-        panel_ref[i, 1] = wi
-        a, b = split(wr)
-        xh[lr:lr + ranks, :] = a
-        xl[lr:lr + ranks, :] = b
-        a, b = split(wi)
-        xh[li:li + ranks, :] = a
-        xl[li:li + ranks, :] = b
-
-    pltpu.make_async_copy(lz, lg.at[h, q], lg_loc.at[0]).wait()
-    each(0, chips, lambda o: rcopy(
-        lz, lg.at[1 - h, o], lg_sib.at[0], lg_recv.at[1 - h, o], sib
-    ).wait_recv())
-
-    def core(k0, carry):
-        k = (k0 + 1) % n_cols
-        j = (c + k) % n_cols
-        lr = lg[0, :, j].reshape(wc, lz.shape[2])
-        li = lg[1, :, j].reshape(wc, lz.shape[2])
-        rank2 = lz.shape[2]
-        uh, ul = split(jnp.concatenate([lr, li], axis=1))
-        prod = dot3(xh[...], xl[...], uh, ul)
-        real = prod[:half, :rank2] - prod[half:, rank2:]
-        imag = prod[:half, rank2:] + prod[half:, :rank2]
-        for i in range(tiles):
-            ks[k, i, 0] = real[i * ranks:(i + 1) * ranks]
-            ks[k, i, 1] = imag[i * ranks:(i + 1) * ranks]
-
-        @pl.when(k > 0)
-        def _():
-            k_out(k).start()
-
-        return carry
-
-    lax.fori_loop(0, n_cols, core, 0)
+    lax.fori_loop(0, total + 1, unit, 0)
     cores_ref[:, 0] = ks[0]
 
     def gather(k):
@@ -303,7 +315,7 @@
         @pl.when(jnp.logical_and(t >= c, d > 0))
         def _():
             for s in range(nsub):
-                u_forward(d, s, t * 2 + h).wait_send()
+                u_forward(t, s, t * 2 + h).wait_send()
 
         @pl.when(t > c)
         def _():
@@ -353,6 +365,8 @@
         scratch_shapes=[
             pltpu.VMEM((m, wc), bf16),
             pltpu.VMEM((m, wc), bf16),
+            pltpu.VMEM((m, wc), bf16),
+            pltpu.VMEM((m, wc), bf16),
             pltpu.VMEM((n_rows, nsub, 2, wc, sw), f32),
             pltpu.VMEM((n_rows, nsub, m, sw), f32),
             pltpu.VMEM((n_rows, nsub, m, sw), f32),

time: 136 us -> 131 us (0.963)
  the two profiles are of different devices: /device:TPU:16 before, /device:TPU:10 now
where the time goes in v2:
time: 131 us
  Pallas kernels  127 us (97%)
  local copies, waits for them, and re-layouts  3.01 us (2%)
    pallas_call x1, Pallas kernels, on_device(): pl.pallas_call(functools.partial(kernel, n_rows, n_cols), out_shape=(jax....  127 us
    unnamed x4, local copies, waits for them, and re-layouts  3.01 us

profile of v2, /device:TPU:10, one launch (start us, length us, event | category | flops | bytes accessed | tf_op | source)
XLA Modules:
  0.0 130.9 jit_solution(12087110542111944953)
XLA Ops:
  0.6 127.3 %shard_map.77 = (f32[2,2,128,512]{3,2,1,0:T(8,128)}, f32[2,1,2,128,128]{4,3,2,1,0:T(8,128)}) custom-call(f32[2,2,128,512]{3,2,1,0:T(8,128)} %row_ref.1, f32[2,512,256]{2,1,0:T(8,128)} %u_ref.1, f32[1,2,2048,128]{3,2,1,0:T(8,128)} %up_ref.1, f32[2,2,512,128]{3,2,1,0:T(8,128)} %col_ref.1, s32[2,128]{1,0:T(2,128)} %piv_ref.1, s32[2]{0:T(128)} %rank_ref.1), custom_call_target="tpu_custom_call" | custom-call | tf_op jit(solution)/shard_map/pallas_call | solution.py:357
  127.9 0.0 copy-start
  127.9 2.3 %copy.10 = f32[2,2,128,512]{3,2,1,0:T(8,128)} copy(f32[2,2,128,512]{3,2,1,0:T(8,128)} %get-tuple-element.4) | data formatting | bytes 2097152
  130.2 0.0 copy-done
  130.2 0.7 copy.11
Async XLA Ops:
  127.9 2.3 %copy-start = (f32[2,1,2,128,128]{4,3,2,1,0:T(8,128)S(1)}, f32[2,1,2,128,128]{4,3,2,1,0:T(8,128)}, u32[]{:S(2)}) copy-start(f32[2,1,2,128,128]{4,3,2,1,0:T(8,128)} %get-tuple-element.5) | copy-start | bytes 786436

commit v3 on v2

--- a/solution.py
+++ b/solution.py
@@ -70,6 +70,10 @@
     def u_forward(t, s, b):
         return rcopy(us.at[b, s], us.at[b, s], u_fwd.at[t, s], u_recv.at[b, s], sib)
 
+    def u_relay(s, b):
+        to = behind(1) if s % 2 == 0 else behind(2)
+        return rcopy(us.at[b, s], us.at[b, s], u_send.at[chips - 1, s], u_recv.at[b, s], (to * 2 + h, c))
+
     def p_up(b, s):
         return rcopy(ps.at[b, s], pr.at[b, s], p_send.at[b, s], p_recv.at[b, s], (r, c + 1))
 
@@ -116,14 +120,16 @@
     each(1, n_cols, lambda k: signal((r, (c + k) % n_cols)))
     pl.semaphore_wait(barrier, 1 + (chips - 1) + (n_cols - 1))
 
-    early = min(3, chips)
+    square = nx == 2 and ny == 2
+    direct = chips - 1 if square else chips
 
     @pl.when(q >= c)
     def _():
         for s in range(nsub):
             u_side(s).start()
 
-        each(1, early, lambda d: u_out(d, 0).start())
+        for s in range(nsub):
+            each(1, direct, lambda d: u_out(d, s).start())
 
     each(1, n_cols, lambda k: lz_out(k).start())
 
@@ -150,7 +156,7 @@
     per = 2 * (chips - 1)
     own_end = 2 * nsub
     last_phase = own_end + (nsub - 1) * per
-    spread_at = jnp.where(c == 0, own_end, 1)
+    spread_at = jnp.where(c == 0, own_end, 0)
     final_at = last_phase + jnp.where(
         q == c, 0, 2 * jnp.where(c > q, chips - 1 - c, chips - 2 - c) + 1
     )
@@ -238,12 +244,6 @@
             pltpu.make_async_copy(lz, lg.at[h, q], lg_loc.at[0]).start()
             each(1, chips, lambda d2: lg_out(d2).start())
 
-            @pl.when(q >= c)
-            def _():
-                each(early, chips, lambda d2: u_out(d2, 0).start())
-                for s2 in range(1, nsub):
-                    each(1, chips, lambda d2: u_out(d2, s2).start())
-
         @pl.when(u == last_phase)
         def _():
             def pass_on(d2):
@@ -262,6 +262,14 @@
             @pl.when(jnp.logical_and(u >= own_end, e == 0))
             def _():
                 u_forward(t, s, b).start()
+
+            if square:
+                for s2 in range(nsub):
+                    source = ahead(2 - s2 % 2)
+
+                    @pl.when(jnp.logical_and(jnp.logical_and(u >= own_end, e == 0), jnp.logical_and(s == s2, t == source)))
+                    def _():
+                        u_relay(s2, source * 2 + h).start()
 
             ur, ui = us[b, s, 0], us[b, s, 1]
             uh, ul = split(jnp.concatenate([ur, ui], axis=1))
@@ -307,7 +315,15 @@
             for s in range(nsub):
                 u_out(d, s).wait_send()
 
-        each(1, chips, left)
+        each(1, direct, left)
+
+    if square:
+        for s in range(nsub):
+            source = ahead(2 - s % 2)
+
+            @pl.when(source >= c)
+            def _():
+                u_relay(s, source * 2 + h).wait_send()
 
     def rest(d):
         t = ahead(d)

time: 131 us -> 139 us (1.061)
  Pallas kernels: 127 us -> 136 us
    pallas_call x1, Pallas kernels: 127 us -> 136 us  [on_device(): pl.pallas_call(functools.partial(kernel, n_rows, n_cols), out_shape=(jax....]
where the time goes in v3:
time: 139 us
  Pallas kernels  136 us (98%)
  local copies, waits for them, and re-layouts  3.01 us (2%)
    pallas_call x1, Pallas kernels, on_device(): pl.pallas_call(functools.partial(kernel, n_rows, n_cols), out_shape=(jax....  136 us
    unnamed x4, local copies, waits for them, and re-layouts  3.01 us

profile of v3, /device:TPU:10, one launch (start us, length us, event | category | flops | bytes accessed | tf_op | source)
XLA Modules:
  0.0 139.2 jit_solution(9837690501759162006)
XLA Ops:
  0.6 135.6 %shard_map.77 = (f32[2,2,128,512]{3,2,1,0:T(8,128)}, f32[2,1,2,128,128]{4,3,2,1,0:T(8,128)}) custom-call(f32[2,2,128,512]{3,2,1,0:T(8,128)} %row_ref.1, f32[2,512,256]{2,1,0:T(8,128)} %u_ref.1, f32[1,2,2048,128]{3,2,1,0:T(8,128)} %up_ref.1, f32[2,2,512,128]{3,2,1,0:T(8,128)} %col_ref.1, s32[2,128]{1,0:T(2,128)} %piv_ref.1, s32[2]{0:T(128)} %rank_ref.1), custom_call_target="tpu_custom_call" | custom-call | tf_op jit(solution)/shard_map/pallas_call | solution.py:373
  136.2 0.0 copy-start
  136.2 2.3 %copy.10 = f32[2,2,128,512]{3,2,1,0:T(8,128)} copy(f32[2,2,128,512]{3,2,1,0:T(8,128)} %get-tuple-element.4) | data formatting | bytes 2097152
  138.5 0.0 copy-done
  138.5 0.7 copy.11
Async XLA Ops:
  136.2 2.3 %copy-start = (f32[2,1,2,128,128]{4,3,2,1,0:T(8,128)S(1)}, f32[2,1,2,128,128]{4,3,2,1,0:T(8,128)}, u32[]{:S(2)}) copy-start(f32[2,1,2,128,128]{4,3,2,1,0:T(8,128)} %get-tuple-element.5) | copy-start | bytes 786436

commit v4 on v2

--- a/solution.py
+++ b/solution.py
@@ -116,14 +116,13 @@
     each(1, n_cols, lambda k: signal((r, (c + k) % n_cols)))
     pl.semaphore_wait(barrier, 1 + (chips - 1) + (n_cols - 1))
 
-    early = min(3, chips)
-
     @pl.when(q >= c)
     def _():
         for s in range(nsub):
             u_side(s).start()
 
-        each(1, early, lambda d: u_out(d, 0).start())
+        for s in range(nsub):
+            each(1, chips, lambda d: u_out(d, s).start())
 
     each(1, n_cols, lambda k: lz_out(k).start())
 
@@ -146,17 +145,19 @@
     for copy in own:
         copy.wait()
 
-    total = chips * nsub * 2
-    per = 2 * (chips - 1)
-    own_end = 2 * nsub
-    last_phase = own_end + (nsub - 1) * per
-    spread_at = jnp.where(c == 0, own_end, 1)
-    final_at = last_phase + jnp.where(
-        q == c, 0, 2 * jnp.where(c > q, chips - 1 - c, chips - 2 - c) + 1
-    )
-    final_at = jnp.where(c == 0, total, final_at)
+    near = chips * (nsub - 1)
+    total = 2 * (near + chips + nsub - 1)
+    spread_at = jnp.where(c == 0, 2, 0)
+    final_at = jnp.where(c == 0, total - 1, 2 * (near + chips - 1 - c) + 1)
 
     def finish():
+        def pass_on(d2):
+            o = ahead(d2)
+            rcopy(lz, lg.at[h, o], lg_send.at[d2], lg_recv.at[h, o], sib).wait_recv()
+            lg_forward(d2).start()
+
+        each(1, chips, pass_on)
+
         each(1, n_cols, lambda k: rcopy(
             eb.at[(c + k) % n_cols], eb.at[(c + k) % n_cols], e_send.at[k], e_recv.at[(c + k) % n_cols], sib
         ).wait_recv())
@@ -219,12 +220,10 @@
         lax.fori_loop(0, n_cols, core, 0)
 
     def unit(u, carry):
-        later = jnp.maximum(u - own_end, 0)
-        index = (later // 2) % (chips - 1)
-        down = chips - 1 - index
-        down = jnp.where(down > q, down, down - 1)
-        t = jnp.where(u < own_end, q, jnp.where(u < last_phase, ahead(index + 1), down))
-        s = jnp.where(u < own_end, u // 2, later // per)
+        slot = u // 2
+        t = jnp.where(slot < near, ahead(slot % chips), jnp.maximum(near + chips - 1 - slot, 0))
+        s = jnp.where(slot < near, slot // chips, jnp.where(slot < near + chips, nsub - 1, slot - near - chips))
+        live = jnp.logical_and(t >= c, jnp.logical_or(slot >= near, t > 0))
         e = u % 2
         b = t * 2 + (h + e) % 2
 
@@ -238,28 +237,13 @@
             pltpu.make_async_copy(lz, lg.at[h, q], lg_loc.at[0]).start()
             each(1, chips, lambda d2: lg_out(d2).start())
 
-            @pl.when(q >= c)
-            def _():
-                each(early, chips, lambda d2: u_out(d2, 0).start())
-                for s2 in range(1, nsub):
-                    each(1, chips, lambda d2: u_out(d2, s2).start())
-
-        @pl.when(u == last_phase)
-        def _():
-            def pass_on(d2):
-                o = ahead(d2)
-                rcopy(lz, lg.at[h, o], lg_send.at[d2], lg_recv.at[h, o], sib).wait_recv()
-                lg_forward(d2).start()
-
-            each(1, chips, pass_on)
-
-        @pl.when(jnp.logical_and(t >= c, u < total))
-        def _():
-            @pl.when(jnp.logical_or(u >= own_end, e > 0))
+        @pl.when(live)
+        def _():
+            @pl.when(jnp.logical_or(t != q, e > 0))
             def _():
                 u_forward(t, s, b).wait_recv()
 
-            @pl.when(jnp.logical_and(u >= own_end, e == 0))
+            @pl.when(jnp.logical_and(t != q, e == 0))
             def _():
                 u_forward(t, s, b).start()
 
@@ -288,7 +272,7 @@
 
         return carry
 
-    lax.fori_loop(0, total + 1, unit, 0)
+    lax.fori_loop(0, total, unit, 0)
     cores_ref[:, 0] = ks[0]
 
     def gather(k):

time: 131 us -> 121 us (0.924)
  the two profiles are of different devices: /device:TPU:10 before, /device:TPU:25 now
where the time goes in v4:
time: 121 us
  Pallas kernels  117 us (97%)
  local copies, waits for them, and re-layouts  3.01 us (2%)
    pallas_call x1, Pallas kernels, on_device(): pl.pallas_call(functools.partial(kernel, n_rows, n_cols), out_shape=(jax....  117 us
    unnamed x4, local copies, waits for them, and re-layouts  3.01 us

profile of v4, /device:TPU:25, one launch (start us, length us, event | category | flops | bytes accessed | tf_op | source)
XLA Modules:
  0.0 120.6 jit_solution(11962935489348992099)
XLA Ops:
  0.6 116.9 %shard_map.77 = (f32[2,2,128,512]{3,2,1,0:T(8,128)}, f32[2,1,2,128,128]{4,3,2,1,0:T(8,128)}) custom-call(f32[2,2,128,512]{3,2,1,0:T(8,128)} %row_ref.1, f32[2,512,256]{2,1,0:T(8,128)} %u_ref.1, f32[1,2,2048,128]{3,2,1,0:T(8,128)} %up_ref.1, f32[2,2,512,128]{3,2,1,0:T(8,128)} %col_ref.1, s32[2,128]{1,0:T(2,128)} %piv_ref.1, s32[2]{0:T(128)} %rank_ref.1), custom_call_target="tpu_custom_call" | custom-call | tf_op jit(solution)/shard_map/pallas_call | solution.py:341
  117.6 0.0 copy-start
  117.6 2.3 %copy.10 = f32[2,2,128,512]{3,2,1,0:T(8,128)} copy(f32[2,2,128,512]{3,2,1,0:T(8,128)} %get-tuple-element.4) | data formatting | bytes 2097152
  119.9 0.0 copy-done
  119.9 0.7 copy.11
Async XLA Ops:
  117.6 2.3 %copy-start = (f32[2,1,2,128,128]{4,3,2,1,0:T(8,128)S(1)}, f32[2,1,2,128,128]{4,3,2,1,0:T(8,128)}, u32[]{:S(2)}) copy-start(f32[2,1,2,128,128]{4,3,2,1,0:T(8,128)} %get-tuple-element.5) | copy-start | bytes 786436

commit v5 on v4

--- a/solution.py
+++ b/solution.py
@@ -122,7 +122,7 @@
             u_side(s).start()
 
         for s in range(nsub):
-            each(1, chips, lambda d: u_out(d, s).start())
+            each(1, chips, lambda d: u_out(d if s == 0 else chips - d, s).start())
 
     each(1, n_cols, lambda k: lz_out(k).start())
 
@@ -133,15 +133,6 @@
             xh[at, :] = a
             xl[at, :] = b
 
-    pos = c * wc + lax.broadcasted_iota(jnp.int32, (wc, ranks), 0)
-    parts = []
-    for i in range(tiles):
-        hit = pos == piv_ref[i:i + 1, :]
-        for p in range(2):
-            parts.append(jnp.sum(jnp.where(hit, col_ref[i, p], 0.0), axis=0, keepdims=True))
-    parts.append(jnp.zeros((eb.shape[1] - 2 * tiles, ranks), jnp.float32))
-    eb[c] = jnp.concatenate(parts, axis=0)
-    each(1, n_cols, lambda k: e_out(k).start())
     for copy in own:
         copy.wait()
 
@@ -198,7 +189,7 @@
         ).wait_recv())
 
         def core(k0, carry):
-            k = (k0 + 1) % n_cols
+            k = jnp.where(c == 0, n_cols - 1 - k0, (k0 + 1) % n_cols)
             j = (c + k) % n_cols
             lr = lg[0, :, j].reshape(wc, lz.shape[2])
             li = lg[1, :, j].reshape(wc, lz.shape[2])
@@ -219,6 +210,17 @@
 
         lax.fori_loop(0, n_cols, core, 0)
 
+    def share():
+        pos = c * wc + lax.broadcasted_iota(jnp.int32, (wc, ranks), 0)
+        parts = []
+        for i in range(tiles):
+            hit = pos == piv_ref[i:i + 1, :]
+            for p in range(2):
+                parts.append(jnp.sum(jnp.where(hit, col_ref[i, p], 0.0), axis=0, keepdims=True))
+        parts.append(jnp.zeros((eb.shape[1] - 2 * tiles, ranks), jnp.float32))
+        eb[c] = jnp.concatenate(parts, axis=0)
+        each(1, n_cols, lambda k: e_out(k).start())
+
     def unit(u, carry):
         slot = u // 2
         t = jnp.where(slot < near, ahead(slot % chips), jnp.maximum(near + chips - 1 - slot, 0))
@@ -236,6 +238,7 @@
             lg_side().start()
             pltpu.make_async_copy(lz, lg.at[h, q], lg_loc.at[0]).start()
             each(1, chips, lambda d2: lg_out(d2).start())
+            share()
 
         @pl.when(live)
         def _():

time: 121 us -> 127 us (1.050)
  Pallas kernels: 117 us -> 122 us
    pallas_call x1, Pallas kernels: 117 us -> 122 us  [on_device(): pl.pallas_call(functools.partial(kernel, n_rows, n_cols), out_shape=(jax....]
where the time goes in v5:
time: 127 us; the launch traced here: 126 us
  Pallas kernels  122 us (96%)
  local copies, waits for them, and re-layouts  3.01 us (2%)
    pallas_call x1, Pallas kernels, on_device(): pl.pallas_call(functools.partial(kernel, n_rows, n_cols), out_shape=(jax....  122 us
    unnamed x4, local copies, waits for them, and re-layouts  3.01 us

profile of v5, /device:TPU:25, one launch (start us, length us, event | category | flops | bytes accessed | tf_op | source)
XLA Modules:
  0.0 125.7 jit_solution(4638074143810023277)
XLA Ops:
  0.6 122.1 %shard_map.77 = (f32[2,2,128,512]{3,2,1,0:T(8,128)}, f32[2,1,2,128,128]{4,3,2,1,0:T(8,128)}) custom-call(f32[2,2,128,512]{3,2,1,0:T(8,128)} %row_ref.1, f32[2,512,256]{2,1,0:T(8,128)} %u_ref.1, f32[1,2,2048,128]{3,2,1,0:T(8,128)} %up_ref.1, f32[2,2,512,128]{3,2,1,0:T(8,128)} %col_ref.1, s32[2,128]{1,0:T(2,128)} %piv_ref.1, s32[2]{0:T(128)} %rank_ref.1), custom_call_target="tpu_custom_call" | custom-call | tf_op jit(solution)/shard_map/pallas_call | solution.py:344
  122.7 0.0 copy-start
  122.7 2.3 %copy.10 = f32[2,2,128,512]{3,2,1,0:T(8,128)} copy(f32[2,2,128,512]{3,2,1,0:T(8,128)} %get-tuple-element.4) | data formatting | bytes 2097152
  125.0 0.0 copy-done
  125.0 0.7 copy.11
Async XLA Ops:
  122.7 2.3 %copy-start = (f32[2,1,2,128,128]{4,3,2,1,0:T(8,128)S(1)}, f32[2,1,2,128,128]{4,3,2,1,0:T(8,128)}, u32[]{:S(2)}) copy-start(f32[2,1,2,128,128]{4,3,2,1,0:T(8,128)} %get-tuple-element.5) | copy-start | bytes 786436

commit v6 on v4

--- a/solution.py
+++ b/solution.py
@@ -70,6 +70,13 @@
     def u_forward(t, s, b):
         return rcopy(us.at[b, s], us.at[b, s], u_fwd.at[t, s], u_recv.at[b, s], sib)
 
+    square = nx == 2 and ny == 2
+    direct = chips - 1 if square else chips
+
+    def u_relay(s, b):
+        to = behind(1) if s % 2 == 0 else behind(2)
+        return rcopy(us.at[b, s], us.at[b, s], u_send.at[chips - 1, s], u_recv.at[b, s], (to * 2 + h, c))
+
     def p_up(b, s):
         return rcopy(ps.at[b, s], pr.at[b, s], p_send.at[b, s], p_recv.at[b, s], (r, c + 1))
 
@@ -122,7 +129,7 @@
             u_side(s).start()
 
         for s in range(nsub):
-            each(1, chips, lambda d: u_out(d, s).start())
+            each(1, direct, lambda d: u_out(d, s).start())
 
     each(1, n_cols, lambda k: lz_out(k).start())
 
@@ -247,6 +254,14 @@
             def _():
                 u_forward(t, s, b).start()
 
+            if square:
+                for s2 in range(nsub):
+                    source = ahead(2 - s2 % 2)
+
+                    @pl.when(jnp.logical_and(e == 0, jnp.logical_and(s == s2, t == source)))
+                    def _():
+                        u_relay(s2, source * 2 + h).start()
+
             ur, ui = us[b, s, 0], us[b, s, 1]
             uh, ul = split(jnp.concatenate([ur, ui], axis=1))
             prod = dot3(xh[...], xl[...], uh, ul)
@@ -291,7 +306,15 @@
             for s in range(nsub):
                 u_out(d, s).wait_send()
 
-        each(1, chips, left)
+        each(1, direct, left)
+
+    if square:
+        for s in range(nsub):
+            source = ahead(2 - s % 2)
+
+            @pl.when(source >= c)
+            def _():
+                u_relay(s, source * 2 + h).wait_send()
 
     def rest(d):
         t = ahead(d)

time: 121 us -> 136 us (1.12)
  Pallas kernels: 117 us -> 132 us
    pallas_call x1, Pallas kernels: 117 us -> 132 us  [on_device(): pl.pallas_call(functools.partial(kernel, n_rows, n_cols), out_shape=(jax....]
where the time goes in v6:
time: 136 us
  Pallas kernels  132 us (97%)
  local copies, waits for them, and re-layouts  3.01 us (2%)
    pallas_call x1, Pallas kernels, on_device(): pl.pallas_call(functools.partial(kernel, n_rows, n_cols), out_shape=(jax....  132 us
    unnamed x4, local copies, waits for them, and re-layouts  3.01 us

profile of v6, /device:TPU:25, one launch (start us, length us, event | category | flops | bytes accessed | tf_op | source)
XLA Modules:
  0.0 135.9 jit_solution(9436530092882797177)
XLA Ops:
  0.6 132.3 %shard_map.77 = (f32[2,2,128,512]{3,2,1,0:T(8,128)}, f32[2,1,2,128,128]{4,3,2,1,0:T(8,128)}) custom-call(f32[2,2,128,512]{3,2,1,0:T(8,128)} %row_ref.1, f32[2,512,256]{2,1,0:T(8,128)} %u_ref.1, f32[1,2,2048,128]{3,2,1,0:T(8,128)} %up_ref.1, f32[2,2,512,128]{3,2,1,0:T(8,128)} %col_ref.1, s32[2,128]{1,0:T(2,128)} %piv_ref.1, s32[2]{0:T(128)} %rank_ref.1), custom_call_target="tpu_custom_call" | custom-call | tf_op jit(solution)/shard_map/pallas_call | solution.py:364
  132.9 0.0 copy-start
  132.9 2.3 %copy.10 = f32[2,2,128,512]{3,2,1,0:T(8,128)} copy(f32[2,2,128,512]{3,2,1,0:T(8,128)} %get-tuple-element.4) | data formatting | bytes 2097152
  135.2 0.0 copy-done
  135.2 0.7 copy.11
Async XLA Ops:
  132.9 2.3 %copy-start = (f32[2,1,2,128,128]{4,3,2,1,0:T(8,128)S(1)}, f32[2,1,2,128,128]{4,3,2,1,0:T(8,128)}, u32[]{:S(2)}) copy-start(f32[2,1,2,128,128]{4,3,2,1,0:T(8,128)} %get-tuple-element.5) | copy-start | bytes 786436

commit v7 on v4

--- a/solution.py
+++ b/solution.py
@@ -121,8 +121,10 @@
         for s in range(nsub):
             u_side(s).start()
 
-        for s in range(nsub):
-            each(1, chips, lambda d: u_out(d, s).start())
+        @pl.when(q > 0)
+        def _():
+            for s in range(nsub):
+                each(1, chips, lambda d: u_out(d, s).start())
 
     each(1, n_cols, lambda k: lz_out(k).start())
 
@@ -198,7 +200,7 @@
         ).wait_recv())
 
         def core(k0, carry):
-            k = (k0 + 1) % n_cols
+            k = jnp.where(c == 0, n_cols - 1 - k0, (k0 + 1) % n_cols)
             j = (c + k) % n_cols
             lr = lg[0, :, j].reshape(wc, lz.shape[2])
             li = lg[1, :, j].reshape(wc, lz.shape[2])
@@ -236,6 +238,11 @@
             lg_side().start()
             pltpu.make_async_copy(lz, lg.at[h, q], lg_loc.at[0]).start()
             each(1, chips, lambda d2: lg_out(d2).start())
+
+            @pl.when(jnp.logical_and(q == 0, q >= c))
+            def _():
+                for s2 in range(nsub):
+                    each(1, chips, lambda d2: u_out(d2, s2).start())
 
         @pl.when(live)
         def _():

time: 121 us -> 117 us (0.967)
  Pallas kernels: 117 us -> 113 us
    pallas_call x1, Pallas kernels: 117 us -> 113 us  [on_device(): pl.pallas_call(functools.partial(kernel, n_rows, n_cols), out_shape=(jax....]
where the time goes in v7:
time: 117 us; the launch traced here: 116 us
  Pallas kernels  113 us (97%)
  local copies, waits for them, and re-layouts  3.01 us (3%)
    pallas_call x1, Pallas kernels, on_device(): pl.pallas_call(functools.partial(kernel, n_rows, n_cols), out_shape=(jax....  113 us
    unnamed x4, local copies, waits for them, and re-layouts  3.01 us

profile of v7, /device:TPU:25, one launch (start us, length us, event | category | flops | bytes accessed | tf_op | source)
XLA Modules:
  0.0 116.4 jit_solution(13430151088155840327)
XLA Ops:
  0.6 112.7 %shard_map.77 = (f32[2,2,128,512]{3,2,1,0:T(8,128)}, f32[2,1,2,128,128]{4,3,2,1,0:T(8,128)}) custom-call(f32[2,2,128,512]{3,2,1,0:T(8,128)} %row_ref.1, f32[2,512,256]{2,1,0:T(8,128)} %u_ref.1, f32[1,2,2048,128]{3,2,1,0:T(8,128)} %up_ref.1, f32[2,2,512,128]{3,2,1,0:T(8,128)} %col_ref.1, s32[2,128]{1,0:T(2,128)} %piv_ref.1, s32[2]{0:T(128)} %rank_ref.1), custom_call_target="tpu_custom_call" | custom-call | tf_op jit(solution)/shard_map/pallas_call | solution.py:348
  113.4 0.0 copy-start
  113.4 2.3 %copy.10 = f32[2,2,128,512]{3,2,1,0:T(8,128)} copy(f32[2,2,128,512]{3,2,1,0:T(8,128)} %get-tuple-element.4) | data formatting | bytes 2097152
  115.7 0.0 copy-done
  115.7 0.7 copy.11
Async XLA Ops:
  113.4 2.3 %copy-start = (f32[2,1,2,128,128]{4,3,2,1,0:T(8,128)S(1)}, f32[2,1,2,128,128]{4,3,2,1,0:T(8,128)}, u32[]{:S(2)}) copy-start(f32[2,1,2,128,128]{4,3,2,1,0:T(8,128)} %get-tuple-element.5) | copy-start | bytes 786436
